TPU v7x, 32 devices: a whole 2x2x4 slice. The times are simulated.
32 devices in a mesh: pipe: 2 (over core), expert: 16 (over z, y, x).
Axes of the slice: x: 2, y: 2, z: 4, core: 2. Of those that a mesh axis runs over, the one named last changes fastest.
Arguments:
- tokens: bfloat16 [2048, 3584], P('expert'), may hold values from -6 to 6
- expert_ids: int32 [2048, 8], P('expert'), may hold values from 0 to 15, all different within a row; in each aligned block of 128 rows (0 to 127, 128 to 255, ...) at most 80 rows name the same one
- combine_weights: float32 [2048, 8], P('expert'), may hold values from 0.1 to 1
- w_gate: bfloat16 [16, 3584, 2048], P('expert', None, 'pipe'), may hold values from -0.09375 to 0.09375
- w_up: bfloat16 [16, 3584, 2048], P('expert', None, 'pipe'), may hold values from -0.09375 to 0.09375
- w_down: bfloat16 [16, 2048, 3584], P('expert', None, 'pipe'), may hold values from -0.125 to 0.125
Outputs:
- mixture: bfloat16 [2048, 3584], P('expert', 'pipe')
Inputs may be any that keep to these rules, and one draw needn't show every extreme that they name: `expert_ids`: each row names 8 different experts. Token t belongs to group t // 128; among the rows of one group no expert is named more than 80 times, and some group names some expert exactly 80 times.
All inputs are finite; a program needn't handle non-finite values.
Results may differ from a plain program's by a relative error of at most 0.0058.
Values may be sent and summed in bfloat16 or wider, within the bound.
A program may use at most 128 MiB of HBM per device.

v0:
```python
import jax
import jax.numpy as jnp
from jax import lax
from jax.sharding import PartitionSpec as P


def body(tokens, expert_ids, combine_weights, w_gate, w_up, w_down):
    experts = lax.axis_size("expert")
    tok_rows, model_width = tokens.shape
    top_count = expert_ids.shape[1]
    capacity = min(tok_rows, 5 * tok_rows * top_count // (4 * experts))
    slot_count = experts * capacity
    hidden_share = w_gate.shape[2]
    out_width = w_down.shape[2]
    expert_iota = lax.broadcasted_iota(jnp.int32, (1, 1, experts), 2)
    chosen = (expert_ids[:, :, None] == expert_iota).astype(jnp.int32)
    expert_hits = jnp.sum(chosen, axis=1)
    rank_table = jnp.cumsum(expert_hits, axis=0) - expert_hits
    slot_rank = jnp.sum(chosen * rank_table[:, None, :], axis=2)
    target = expert_ids * capacity + slot_rank
    slot_iota = lax.broadcasted_iota(jnp.int32, (1, 1, slot_count), 2)
    slot_marks = target[:, :, None] == slot_iota
    placing = jnp.any(slot_marks, axis=1).astype(jnp.bfloat16)
    blend_table = jnp.sum(jnp.where(slot_marks, combine_weights[:, :, None], 0.0), axis=1)
    packed = jnp.einsum("ts,td->sd", placing, tokens, preferred_element_type=jnp.float32)
    packed = packed.astype(jnp.bfloat16).reshape(experts, capacity, model_width)
    received = lax.all_to_all(packed, "expert", split_axis=0, concat_axis=0, tiled=True)
    gate_acc = jnp.einsum("scd,df->scf", received, w_gate[0], preferred_element_type=jnp.float32)
    up_acc = jnp.einsum("scd,df->scf", received, w_up[0], preferred_element_type=jnp.float32)
    hidden = (jax.nn.silu(gate_acc) * up_acc).astype(jnp.bfloat16)
    hidden_rows = hidden.reshape(slot_count, hidden_share)
    down_rows = w_down[0]
    outputs = jnp.dot(
        lax.all_gather(hidden_rows, "pipe", axis=1, tiled=True),
        down_rows,
        preferred_element_type=jnp.float32,
    )
    outgoing = outputs.astype(jnp.bfloat16).reshape(experts, capacity, out_width)
    returned_rows = lax.all_to_all(outgoing, "expert", split_axis=0, concat_axis=0, tiled=True)
    mixture = jnp.dot(
        blend_table,
        returned_rows.reshape(slot_count, out_width).astype(jnp.float32),
        precision=lax.Precision.HIGHEST,
        preferred_element_type=jnp.float32,
    )
    return mixture.astype(jnp.bfloat16)


def solution(mesh):
    placed = (
        P("expert", None),
        P("expert", None),
        P("expert", None),
        P("expert", None, "pipe"),
        P("expert", None, "pipe"),
        P("expert", None, "pipe"),
    )
    return jax.shard_map(
        body, mesh=mesh, in_specs=placed, out_specs=P("expert", "pipe"), check_vma=False
    )
```

profile of v0, /device:TPU:14, one launch (start us, length us, event | category | flops | bytes accessed | tf_op | source)
XLA Modules:
  0.0 396.9 jit_solution(9691177546608516601)
XLA Ops:
  6.5 0.0 copy-start
  6.5 0.0 all-gather.2.cloned.1.call-start
  6.5 0.8 convert_reduce_fusion
  7.3 0.1 copy.10
  7.4 0.2 reduce_window_sum.11
  7.6 0.1 copy.12
  7.7 0.7 select_reduce_fusion.1
  8.4 0.7 multiply_add_fusion
  9.1 0.1 copy.13
  9.2 1.6 fusion.5
  10.8 0.0 copy-done
  10.8 0.0 slice-start
  10.9 2.6 convolution_convert_fusion
  13.4 0.0 slice-start.1
  13.5 205.6 %all_to_all.10 = bf16[16,80,3584]{2,1,0:T(8,128)(2,1)S(1)} all-to-all(bf16[16,80,3584]{2,1,0:T(8,128)(2,1)S(1)} %bitcast.24), channel_id=1, replica_groups=mesh['pipe'=2,'expert'=16] {'expert'}, dimensions={0} | all-to-all | bytes 18350080 | tf_op jit(solution)/shard_map/all_to_all | solution.py:27
  219.1 0.0 slice-done
  219.1 0.0 slice-done.1
  219.1 9.7 %fusion.1 = f32[16,80,1024]{2,1,0:T(8,128)S(1)} fusion(bf16[16,80,3584]{2,1,0:T(8,128)(2,1)S(1)} %all_to_all.10, bf16[1,3584,1024]{2,1,0:T(8,128)(2,1)S(1)} %bitcast.28), kind=kOutput, calls=%fused_computation.3 | convolution fusion | flops 9395240960 | bytes 21757952 | tf_op jit(solution)/shard_map/scd,df->scf/dot_general | solution.py:29
  228.7 13.9 %multiply_convert_fusion = bf16[16,80,1024]{2,1,0:T(8,128)(2,1)} fusion(f32[16,80,1024]{2,1,0:T(8,128)S(1)} %fusion.1, bf16[16,80,3584]{2,1,0:T(8,128)(2,1)S(1)} %all_to_all.10, bf16[1,3584,1024]{2,1,0:T(8,128)(2,1)} %param.9), kind=kOutput, calls=%fused_computation.7 | convolution fusion | flops 9403105280 | bytes 24379392 | tf_op jit(solution)/shard_map/scd,df->scf/dot_general | solution.py:28
  242.6 0.0 all-gather.2.cloned.1.call-update
  242.7 15.6 %all-gather.2.cloned.1.call-done = bf16[1280,2048]{1,0:T(8,128)(2,1)} async-done(((bf16[1280,1024]{1,0:T(8,128)(2,1)}), bf16[1280,2048]{1,0:T(8,128)(2,1)}) %all-gather.2.cloned.1.call-update) | async-done | bytes 5242896 | tf_op jit(solution)/shard_map/all_gather | solution.py:34
  258.3 15.1 %convolution_convert_fusion.1 = bf16[1280,1792]{1,0:T(8,128)(2,1)} fusion(bf16[1280,2048]{1,0:T(8,128)(2,1)} %all-gather.2.cloned.1.call-done, bf16[1,2048,1792]{2,1,0:T(8,128)(2,1)} %param.11), kind=kOutput, calls=%fused_computation.1 | convolution fusion | flops 9397534720 | bytes 17170432 | tf_op jit(solution)/shard_map/dot_general | solution.py:33
  273.4 0.0 copy-start.1
  273.4 7.1 %all-to-all-start.1 = ((bf16[16,80,1792]{2,1,0:T(8,128)(2,1)}), bf16[16,80,1792]{2,1,0:T(8,128)(2,1)}, u32[]{:S(2)}, u32[]{:S(2)}) async-start(bf16[16,80,1792]{2,1,0:T(8,128)(2,1)} %bitcast.25), calls=%async_computation.1 | async-start | bytes 9175040 | tf_op jit(solution)/shard_map/all_to_all | solution.py:39
  280.5 0.0 copy-done.1
  280.5 0.1 copy.14
  280.6 1.6 select_reduce_fusion
  282.2 102.8 %all-to-all-done.1 = bf16[16,80,1792]{2,1,0:T(8,128)(2,1)} async-done(((bf16[16,80,1792]{2,1,0:T(8,128)(2,1)}), bf16[16,80,1792]{2,1,0:T(8,128)(2,1)}, u32[]{:S(2)}, u32[]{:S(2)}) %all-to-all-start.1) | async-done | bytes 4587552 | tf_op jit(solution)/shard_map/all_to_all | solution.py:39
  385.0 5.0 %convolution_convert_fusion.2 = bf16[128,1792]{1,0:T(8,128)(2,1)} fusion(f32[128,1280]{1,0:T(8,128)S(1)} %select_reduce_fusion, bf16[1280,1792]{1,0:T(8,128)(2,1)} %bitcast.8), kind=kOutput, calls=%fused_computation.11 | convolution fusion | flops 3523444736 | bytes 5701632 | tf_op jit(solution)/shard_map/dot_general | solution.py:40
  (2 shorter events, 0.0 us)
Async XLA Ops:
  6.5 4.3 %copy-start = (bf16[128,3584]{1,0:T(8,128)(2,1)S(1)}, bf16[128,3584]{1,0:T(8,128)(2,1)}, u32[]{:S(2)}) copy-start(bf16[128,3584]{1,0:T(8,128)(2,1)} %param.6) | copy-start | bytes 2752516
  6.5 251.7 %all-gather.2.cloned.1.call-start = ((), (), s32[]{:S(2)}) async-start(), calls=%async_computation.2 | async-start | bytes 7864320 | tf_op jit(solution)/shard_map/all_gather | solution.py:34
  10.8 208.2 %slice-start = ((s8[7340032]{0:T(1024)(128)(4,1)}), s8[4194304]{0:T(1024)(128)(4,1)S(1)}, s32[]{:S(2)}) async-start(s8[7340032]{0:T(1024)(128)(4,1)} %bitcast.27), calls=%async_computation.3 | async-start | bytes 8388608
  13.4 205.6 %slice-start.1 = ((s8[7340032]{0:T(1024)(128)(4,1)}), s8[3145728]{0:T(1024)(128)(4,1)S(1)}, s32[]{:S(2)}) async-start(s8[7340032]{0:T(1024)(128)(4,1)} %bitcast.27), calls=%async_computation.4 | async-start | bytes 6291456
  273.4 7.1 %copy-start.1 = (f32[128,8]{0,1:T(8,128)S(1)}, f32[128,8]{0,1:T(8,128)}, u32[]{:S(2)}) copy-start(f32[128,8]{0,1:T(8,128)} %param.8) | copy-start | bytes 12292
  273.4 111.6 %all-to-all-start.1 = ((bf16[16,80,1792]{2,1,0:T(8,128)(2,1)}), bf16[16,80,1792]{2,1,0:T(8,128)(2,1)}, u32[]{:S(2)}, u32[]{:S(2)}) async-start(bf16[16,80,1792]{2,1,0:T(8,128)(2,1)} %bitcast.25), calls=%async_computation.1 | async-start | bytes 9175040 | tf_op jit(solution)/shard_map/all_to_all | solution.py:39
Sparse Core Ops, SparseCore 0:
  242.8 15.4 all-gather.1
where the time goes:
time: 397 us
  blocking collectives  206 us (52%)
  waiting for transfers between devices  118 us (30%)
  matrix products  46.3 us (12%)
  between operations  13.5 us (3%)
  starting transfers between devices  7.09 us (2%)
  other arithmetic  5.64 us (1%)
    all_to_all x1, blocking collectives, body(): lax.all_to_all(packed, 'expert', split_axis=0, concat_axis=0, tiled=True)  206 us
    all_to_all x1, waiting for transfers between devices, body(): lax.all_to_all(outgoing, 'expert', split_axis=0, concat_axis=0, tiled=True)  103 us
    all_gather x1, waiting for transfers between devices, body(): lax.all_gather(hidden_rows, 'pipe', axis=1, tiled=True)  15.6 us
    dot_general x1, matrix products, body(): jnp.dot(lax.all_gather(hidden_rows, 'pipe', axis=1, tiled=True), down_row...  15.1 us
    dot_general x1, matrix products, body(): jnp.einsum('scd,df->scf', received, w_gate[0], preferred_element_type=jnp...  13.9 us
    dot_general x1, matrix products, body(): jnp.einsum('scd,df->scf', received, w_up[0], preferred_element_type=jnp.f...  9.66 us
  transfers between devices with their start and end apart: 2, of which 2 were waited for; matrix products, arithmetic and copies ran while one was open for 0% of the time, Pallas kernels for 0%

commit v1 on v0

--- a/solution.py
+++ b/solution.py
@@ -2,6 +2,19 @@
 import jax.numpy as jnp
 from jax import lax
 from jax.sharding import PartitionSpec as P
+
+
+def split_dots(mine, weights):
+    place = lax.axis_index("pipe")
+    other = lax.ppermute(mine, "pipe", [(0, 1), (1, 0)])
+    share = mine.shape[1]
+    totals = []
+    for weight in weights:
+        own = lax.dynamic_slice_in_dim(weight, place * share, share, 0)
+        far = lax.dynamic_slice_in_dim(weight, (1 - place) * share, share, 0)
+        total = jnp.dot(mine, own, preferred_element_type=jnp.float32)
+        totals.append(total + jnp.dot(other, far, preferred_element_type=jnp.float32))
+    return totals
 
 
 def body(tokens, expert_ids, combine_weights, w_gate, w_up, w_down):
@@ -10,7 +23,6 @@
     top_count = expert_ids.shape[1]
     capacity = min(tok_rows, 5 * tok_rows * top_count // (4 * experts))
     slot_count = experts * capacity
-    hidden_share = w_gate.shape[2]
     out_width = w_down.shape[2]
     expert_iota = lax.broadcasted_iota(jnp.int32, (1, 1, experts), 2)
     chosen = (expert_ids[:, :, None] == expert_iota).astype(jnp.int32)
@@ -22,19 +34,29 @@
     slot_marks = target[:, :, None] == slot_iota
     placing = jnp.any(slot_marks, axis=1).astype(jnp.bfloat16)
     blend_table = jnp.sum(jnp.where(slot_marks, combine_weights[:, :, None], 0.0), axis=1)
-    packed = jnp.einsum("ts,td->sd", placing, tokens, preferred_element_type=jnp.float32)
-    packed = packed.astype(jnp.bfloat16).reshape(experts, capacity, model_width)
+    pipes = lax.axis_size("pipe")
+    place = lax.axis_index("pipe")
+    width_share = model_width // pipes
+    tok_share = lax.dynamic_slice_in_dim(tokens, place * width_share, width_share, 1)
+    packed = jnp.einsum("ts,td->sd", placing, tok_share, preferred_element_type=jnp.float32)
+    packed = packed.astype(jnp.bfloat16).reshape(experts, capacity, width_share)
     received = lax.all_to_all(packed, "expert", split_axis=0, concat_axis=0, tiled=True)
-    gate_acc = jnp.einsum("scd,df->scf", received, w_gate[0], preferred_element_type=jnp.float32)
-    up_acc = jnp.einsum("scd,df->scf", received, w_up[0], preferred_element_type=jnp.float32)
-    hidden = (jax.nn.silu(gate_acc) * up_acc).astype(jnp.bfloat16)
-    hidden_rows = hidden.reshape(slot_count, hidden_share)
-    down_rows = w_down[0]
-    outputs = jnp.dot(
-        lax.all_gather(hidden_rows, "pipe", axis=1, tiled=True),
-        down_rows,
-        preferred_element_type=jnp.float32,
-    )
+    rows = received.reshape(slot_count, width_share)
+    if pipes == 2:
+        gate_acc, up_acc = split_dots(rows, [w_gate[0], w_up[0]])
+    else:
+        rows = lax.all_gather(rows, "pipe", axis=1, tiled=True)
+        gate_acc = jnp.dot(rows, w_gate[0], preferred_element_type=jnp.float32)
+        up_acc = jnp.dot(rows, w_up[0], preferred_element_type=jnp.float32)
+    hidden_rows = (jax.nn.silu(gate_acc) * up_acc).astype(jnp.bfloat16)
+    if pipes == 2:
+        (outputs,) = split_dots(hidden_rows, [w_down[0]])
+    else:
+        outputs = jnp.dot(
+            lax.all_gather(hidden_rows, "pipe", axis=1, tiled=True),
+            w_down[0],
+            preferred_element_type=jnp.float32,
+        )
     outgoing = outputs.astype(jnp.bfloat16).reshape(experts, capacity, out_width)
     returned_rows = lax.all_to_all(outgoing, "expert", split_axis=0, concat_axis=0, tiled=True)
     mixture = jnp.dot(

time: 397 us -> 284 us (0.72)
  blocking collectives: 206 us -> 107 us
  waiting for transfers between devices: 118 us -> 103 us
  matrix products: 46.3 us -> 59.9 us
  between operations: 13.5 us -> 0.15 us
    all_to_all x1, blocking collectives: 206 us -> 107 us  [body(): lax.all_to_all(packed, 'expert', split_axis=0, concat_axis=0, tiled=True)]
    all_gather x1 -> x0, waiting for transfers between devices: 15.6 us -> none  [body(): lax.all_gather(hidden_rows, 'pipe', axis=1, tiled=True)]
    dot_general x4 -> x7, matrix products: 41.3 us -> 54.9 us  [the longest x3 29.7 us: split_dots(): jnp.dot(other, far, preferred_element_type=jnp.float32)]
  transfers between devices with their start and end apart: 2 -> 3, of which waited for: 2 -> 1; matrix products, arithmetic and copies ran while one was open for 0% -> 9% of each run, Pallas kernels for 0% -> 0%
where the time goes in v1:
time: 284 us; the launch traced here: 283 us
  blocking collectives  107 us (38%)
  waiting for transfers between devices  103 us (36%)
  matrix products  59.9 us (21%)
  starting transfers between devices  7.46 us (3%)
  other arithmetic  5.64 us (2%)
    all_to_all x1, blocking collectives, body(): lax.all_to_all(packed, 'expert', split_axis=0, concat_axis=0, tiled=True)  107 us
    all_to_all x1, waiting for transfers between devices, body(): lax.all_to_all(outgoing, 'expert', split_axis=0, concat_axis=0, tiled=True)  103 us
    dot_general x3, matrix products, split_dots(): jnp.dot(other, far, preferred_element_type=jnp.float32)  29.7 us
    dot_general x3, matrix products, split_dots(): total = jnp.dot(mine, own, preferred_element_type=jnp.float32)  23.7 us
    all_to_all x1, starting transfers between devices, body(): lax.all_to_all(outgoing, 'expert', split_axis=0, concat_axis=0, tiled=True)  6.95 us
  transfers between devices with their start and end apart: 3, of which 1 were waited for; matrix products, arithmetic and copies ran while one was open for 9% of the time, Pallas kernels for 0%

profile of v1, /device:TPU:14, one launch (start us, length us, event | category | flops | bytes accessed | tf_op | source)
XLA Modules:
  0.0 283.4 jit_solution(10538882112971376323)
XLA Ops:
  0.0 0.0 copy-start
  0.0 0.8 convert_reduce_fusion
  0.8 0.1 copy.10
  0.9 0.2 reduce_window_sum.11
  1.1 0.1 copy.12
  1.1 0.7 select_reduce_fusion.1
  1.9 0.7 multiply_add_fusion
  2.5 0.1 copy.13
  2.7 1.6 fusion
  4.3 0.0 copy-done
  4.3 1.4 convolution_convert_fusion
  5.7 107.1 %all_to_all.10 = bf16[16,80,1792]{2,1,0:T(8,128)(2,1)} all-to-all(bf16[16,80,1792]{2,1,0:T(8,128)(2,1)S(1)} %bitcast.31), channel_id=1, replica_groups=mesh['pipe'=2,'expert'=16] {'expert'}, dimensions={0} | all-to-all | bytes 9175040 | tf_op jit(solution)/shard_map/all_to_all | solution.py:43
  112.9 0.0 collective-permute-start
  112.9 8.0 %fusion.5 = f32[1280,1024]{1,0:T(8,128)S(1)} fusion(bf16[1280,1792]{1,0:T(8,128)(2,1)} %bitcast.1, bf16[1,3584,1024]{2,1,0:T(8,128)(2,1)} %param.10, s32[]{:T(128)S(6)} %select_n.20), kind=kOutput, calls=%fused_computation.10 | convolution fusion | flops 4697620480 | bytes 13500420 | tf_op jit(solution)/shard_map/dot_general | solution.py:15
  120.8 0.0 slice-start.1
  120.8 0.0 slice-start.2
  120.9 8.0 %fusion.9 = f32[1280,1024]{1,0:T(8,128)S(1)} fusion(bf16[1280,1792]{1,0:T(8,128)(2,1)} %bitcast.1, bf16[1,3584,1024]{2,1,0:T(8,128)(2,1)} %param.9, s32[]{:T(128)S(6)} %select_n.20), kind=kOutput, calls=%fused_computation.14 | convolution fusion | flops 4697620480 | bytes 13500420 | tf_op jit(solution)/shard_map/dot_general | solution.py:15
  128.8 0.0 slice-start.3
  128.9 0.0 collective-permute-done
  128.9 9.1 %fusion.7 = f32[1280,1024]{1,0:T(8,128)} fusion(bf16[1280,1792]{1,0:T(8,128)(2,1)} %collective-permute-done, bf16[1,3584,1024]{2,1,0:T(8,128)(2,1)S(1)} %bitcast.34, s32[]{:T(128)S(6)} %select_n.21), kind=kOutput, calls=%fused_computation.12 | convolution fusion | flops 4697620480 | bytes 13500420 | tf_op jit(solution)/shard_map/dot_general | solution.py:16
  138.1 10.5 %multiply_convert_fusion = bf16[1280,1024]{1,0:T(8,128)(2,1)} fusion(f32[1280,1024]{1,0:T(8,128)S(1)} %fusion.5, f32[1280,1024]{1,0:T(8,128)S(1)} %fusion.9, f32[1280,1024]{1,0:T(8,128)} %fusion.7, bf16[1280,1792]{1,0:T(8,128)(2,1)} %collective-permute-done, bf16[1,3584,1024]{2,1,0:T(8,128)(2,1)S(1)} %bitcast.36, s32[]{:T(128)S(6)} %select_n.21), kind=kOutput, calls=%fused_computation.2 | convolution fusion | flops 4708106240 | bytes 26607620 | tf_op jit(solution)/shard_map/dot_general | solution.py:16
  148.6 0.5 collective-permute-start.1
  149.1 7.8 %fusion.2 = f32[1280,1792]{1,0:T(8,128)S(1)} fusion(bf16[1280,1024]{1,0:T(8,128)(2,1)} %multiply_convert_fusion, bf16[1,2048,1792]{2,1,0:T(8,128)(2,1)} %param.11, s32[]{:T(128)S(6)} %select_n.22), kind=kOutput, calls=%fused_computation.7 | convolution fusion | flops 4697620480 | bytes 15466500 | tf_op jit(solution)/shard_map/dot_general | solution.py:15
  156.9 0.0 collective-permute-done.1
  156.9 10.1 %add_convert_fusion = bf16[1280,1792]{1,0:T(8,128)(2,1)} fusion(f32[1280,1792]{1,0:T(8,128)S(1)} %fusion.2, bf16[1280,1024]{1,0:T(8,128)(2,1)} %collective-permute-done.1, bf16[1,2048,1792]{2,1,0:T(8,128)(2,1)} %param.11, s32[]{:T(128)S(6)} %select_n.23), kind=kOutput, calls=%fused_computation | convolution fusion | flops 4702208000 | bytes 20054020 | tf_op jit(solution)/shard_map/dot_general | solution.py:16
  167.0 6.9 %all-to-all-start.1 = ((bf16[16,80,1792]{2,1,0:T(8,128)(2,1)}), bf16[16,80,1792]{2,1,0:T(8,128)(2,1)}, u32[]{:S(2)}, u32[]{:S(2)}) async-start(bf16[16,80,1792]{2,1,0:T(8,128)(2,1)} %bitcast.32), calls=%async_computation.1 | async-start | bytes 9175040 | tf_op jit(solution)/shard_map/all_to_all | solution.py:61
  173.9 0.0 copy-start.1
  173.9 0.1 copy.14
  174.0 1.6 select_reduce_fusion
  175.7 102.7 %all-to-all-done.1 = bf16[16,80,1792]{2,1,0:T(8,128)(2,1)} async-done(((bf16[16,80,1792]{2,1,0:T(8,128)(2,1)}), bf16[16,80,1792]{2,1,0:T(8,128)(2,1)}, u32[]{:S(2)}, u32[]{:S(2)}) %all-to-all-start.1) | async-done | bytes 4587552 | tf_op jit(solution)/shard_map/all_to_all | solution.py:61
  278.4 5.0 %convolution_convert_fusion.1 = bf16[128,1792]{1,0:T(8,128)(2,1)} fusion(f32[128,1280]{1,0:T(8,128)S(1)} %select_reduce_fusion, bf16[1280,1792]{1,0:T(8,128)(2,1)} %bitcast.9), kind=kOutput, calls=%fused_computation.22 | convolution fusion | flops 3523444736 | bytes 5701632 | tf_op jit(solution)/shard_map/dot_general | solution.py:62
  283.4 0.0 copy-done.1
  (10 shorter events, 0.0 us)
Async XLA Ops:
  0.0 4.3 %copy-start = (bf16[128,3584]{1,0:T(8,128)(2,1)S(1)}, bf16[128,3584]{1,0:T(8,128)(2,1)}, u32[]{:S(2)}) copy-start(bf16[128,3584]{1,0:T(8,128)(2,1)} %param.6) | copy-start | bytes 2752516
  112.9 16.0 %collective-permute-start = (bf16[1280,1792]{1,0:T(8,128)(2,1)}, bf16[1280,1792]{1,0:T(8,128)(2,1)}, u32[]{:S(2)}, u32[]{:S(2)}) collective-permute-start(bf16[1280,1792]{1,0:T(8,128)(2,1)} %bitcast.1), channel_id=1, source_target_pairs={{0,16},{16,0},{1,17},{17,1},{2,18},{18,2},{3,19},{19,3},{4,20},{20... | collective-permute-start | bytes 13762568 | tf_op jit(solution)/shard_map/ppermute | solution.py:9
  112.9 16.0 %slice-start = ((s8[7340032]{0:T(1024)(128)(4,1)}), s8[4194304]{0:T(1024)(128)(4,1)S(1)}, s32[]{:S(2)}) async-start(s8[7340032]{0:T(1024)(128)(4,1)} %bitcast.33), calls=%async_computation.2 | async-start | bytes 8388608
  120.8 8.0 %slice-start.1 = ((s8[7340032]{0:T(1024)(128)(4,1)}), s8[3145728]{0:T(1024)(128)(4,1)S(1)}, s32[]{:S(2)}) async-start(s8[7340032]{0:T(1024)(128)(4,1)} %bitcast.33), calls=%async_computation.3 | async-start | bytes 6291456
  120.8 17.2 %slice-start.2 = ((s8[7340032]{0:T(1024)(128)(4,1)}), s8[4194304]{0:T(1024)(128)(4,1)S(1)}, s32[]{:S(2)}) async-start(s8[7340032]{0:T(1024)(128)(4,1)} %bitcast.35), calls=%async_computation.4 | async-start | bytes 8388608
  128.8 9.2 %slice-start.3 = ((s8[7340032]{0:T(1024)(128)(4,1)}), s8[3145728]{0:T(1024)(128)(4,1)S(1)}, s32[]{:S(2)}) async-start(s8[7340032]{0:T(1024)(128)(4,1)} %bitcast.35), calls=%async_computation.5 | async-start | bytes 6291456
  148.6 8.3 %collective-permute-start.1 = (bf16[1280,1024]{1,0:T(8,128)(2,1)}, bf16[1280,1024]{1,0:T(8,128)(2,1)}, u32[]{:S(2)}, u32[]{:S(2)}) collective-permute-start(bf16[1280,1024]{1,0:T(8,128)(2,1)} %multiply_convert_fusion), channel_id=1, source_target_pairs={{0,16},{16,0},{1,17},{17,1},{2,18},{18,2},{3,19},{19,3},{4,20},{20... | collective-permute-start | bytes 7864328 | tf_op jit(solution)/shard_map/ppermute | solution.py:9
  167.0 7.0 %copy-start.2 = (f32[128,8]{0,1:T(8,128)S(1)}, f32[128,8]{0,1:T(8,128)}, u32[]{:S(2)}) copy-start(f32[128,8]{0,1:T(8,128)} %param.8) | copy-start | bytes 12292
  167.0 111.4 %all-to-all-start.1 = ((bf16[16,80,1792]{2,1,0:T(8,128)(2,1)}), bf16[16,80,1792]{2,1,0:T(8,128)(2,1)}, u32[]{:S(2)}, u32[]{:S(2)}) async-start(bf16[16,80,1792]{2,1,0:T(8,128)(2,1)} %bitcast.32), calls=%async_computation.1 | async-start | bytes 9175040 | tf_op jit(solution)/shard_map/all_to_all | solution.py:61
  173.9 109.5 %copy-start.1 = (bf16[128,3584]{1,0:T(8,128)(2,1)S(1)}, bf16[128,3584]{1,0:T(8,128)(2,1)}, u32[]{:S(2)}) copy-start(bf16[128,3584]{1,0:T(8,128)(2,1)} %param.6) | copy-start | bytes 2752516

commit v2 on v1

--- a/solution.py
+++ b/solution.py
@@ -1,7 +1,244 @@
 import jax
 import jax.numpy as jnp
 from jax import lax
+from jax.experimental import pallas as pl
+from jax.experimental.pallas import tpu as pltpu
 from jax.sharding import PartitionSpec as P
+
+LAYERS, SIDE = 4, 2
+MESH = pl.DeviceIdType.MESH
+
+
+def grid_place():
+    me = lax.axis_index("expert")
+    return me // 4, lax.rem(me // 2, 2), lax.rem(me, 2)
+
+
+def flat_place(z, y, x):
+    return z * 4 + y * 2 + x
+
+
+def greet():
+    z, y, x = grid_place()
+    barrier = pltpu.get_barrier_semaphore()
+    partners = [flat_place(lax.rem(z + k, LAYERS), y, x) for k in range(1, LAYERS)]
+    partners += [flat_place(z, 1 - y, x), flat_place(z, y, 1 - x)]
+    for partner in partners:
+        pl.semaphore_signal(barrier, inc=1, device_id={"expert": partner}, device_id_type=MESH)
+    pl.semaphore_wait(barrier, len(partners))
+
+
+def gather_kernel(tok_ref, table_ref, out_ref, tables_ref, send_sem, recv_sem, local_sem):
+    z, y, x = grid_place()
+    me = flat_place(z, y, x)
+    greet()
+    own = [tok_ref.at[0], tok_ref.at[1], table_ref]
+    slots = [lambda e: out_ref.at[e, 0], lambda e: out_ref.at[e, 1], lambda e: tables_ref.at[e]]
+    hops = [
+        (flat_place(z, 1 - y, x), flat_place(z, y, 1 - x)),
+        (flat_place(z, y, 1 - x), flat_place(z, 1 - y, x)),
+        (flat_place(z, 1 - y, x), flat_place(z, y, 1 - x)),
+    ]
+    kept = [pltpu.make_async_copy(own[j], slots[j](me), local_sem.at[j]) for j in range(3)]
+    started = []
+
+    def send(source, slot, partner, j, k, step):
+        copy = pltpu.make_async_remote_copy(
+            src_ref=source, dst_ref=slot, send_sem=send_sem.at[j, k, step],
+            recv_sem=recv_sem.at[j, k, step], device_id={"expert": partner}, device_id_type=MESH,
+        )
+        copy.start()
+        started.append(copy)
+        return copy
+
+    order = (2, 0, 1)
+    along = {}
+    for k in range(1, LAYERS):
+        for j in order:
+            along[j, k] = send(own[j], slots[j](me), flat_place(lax.rem(z + k, LAYERS), y, x), j, k, 0)
+    near = {}
+
+    def spread(k):
+        origin = flat_place(lax.rem(z - k + LAYERS, LAYERS), y, x)
+        for j in order:
+            if k:
+                along[j, k].wait_recv()
+            source = slots[j](origin) if k else own[j]
+            near[j, k] = send(source, slots[j](origin), hops[j][0], j, k, 1)
+            send(source, slots[j](origin), hops[j][1], j, k, 2)
+
+    def forward(k):
+        layer = lax.rem(z - k + LAYERS, LAYERS)
+        for j in order:
+            origin = flat_place(layer, y, 1 - x) if j == 1 else flat_place(layer, 1 - y, x)
+            near[j, k].wait_recv()
+            send(slots[j](origin), slots[j](origin), hops[j][1], j, k, 3)
+
+    spread(0)
+    for copy in kept:
+        copy.start()
+    for k in range(1, LAYERS):
+        spread(k)
+        forward(k - 1)
+    forward(LAYERS - 1)
+    for copy in kept:
+        copy.wait()
+    for copy in started:
+        copy.wait_send()
+    waited = list(along.values()) + list(near.values())
+    for copy in started:
+        if not any(copy is other for other in waited):
+            copy.wait_recv()
+
+
+def gather_rows(tokens, table):
+    rows, width = tokens.shape
+    experts = lax.axis_size("expert")
+    half = rows // 2
+    anywhere = pl.BlockSpec(memory_space=pl.ANY)
+    gathered, tables = pl.pallas_call(
+        gather_kernel,
+        out_shape=(
+            jax.ShapeDtypeStruct((experts, 2, half, width), tokens.dtype),
+            jax.ShapeDtypeStruct((experts, rows, table.shape[1]), table.dtype),
+        ),
+        in_specs=[anywhere, anywhere],
+        out_specs=(anywhere, anywhere),
+        scratch_shapes=[
+            pltpu.SemaphoreType.DMA((3, LAYERS, 4)),
+            pltpu.SemaphoreType.DMA((3, LAYERS, 4)),
+            pltpu.SemaphoreType.DMA((3,)),
+        ],
+        compiler_params=pltpu.CompilerParams(collective_id=0, has_side_effects=True),
+    )(tokens.reshape(2, half, width), table)
+    return gathered.reshape(experts, rows, width), tables
+
+
+def reduce_kernel(part_ref, out_ref, first, second, last, send1, recv1, send2, recv2, send3, recv3):
+    z, y, x = grid_place()
+    greet()
+
+    def target(k, h, far_first, far_second):
+        layer = lax.rem(z + k, LAYERS)
+        flip_y, flip_x = (far_second, far_first) if h == 0 else (far_first, far_second)
+        return flat_place(layer, 1 - y if flip_y else y, 1 - x if flip_x else x)
+
+    def send(source, slot, partner, send_sem, recv_sem):
+        copy = pltpu.make_async_remote_copy(
+            src_ref=source, dst_ref=slot, send_sem=send_sem, recv_sem=recv_sem,
+            device_id={"expert": partner}, device_id_type=MESH,
+        )
+        copy.start()
+        return copy
+
+    wide = jnp.float32
+    order = (2, 1, 3, 0)
+    one, two, three = {}, {}, {}
+    for k in order:
+        for j in range(2):
+            for h in range(2):
+                one[h, k, j] = send(
+                    part_ref.at[target(k, h, True, j == 0), h], first.at[h, k, j],
+                    target(0, h, True, False), send1.at[h, k, j], recv1.at[h, k, j],
+                )
+
+    def pass_on(k):
+        for h in range(2):
+            one[h, k, 0].wait_recv()
+            mine = part_ref[target(k, h, False, True), h].astype(wide)
+            first[h, k, 0] = (mine + first[h, k, 0].astype(wide)).astype(first.dtype)
+            two[h, k] = send(
+                first.at[h, k, 0], second.at[h, k], target(0, h, False, True),
+                send2.at[h, k], recv2.at[h, k],
+            )
+
+    def total(k, h):
+        one[h, k, 1].wait_recv()
+        two[h, k].wait_recv()
+        mine = part_ref[target(k, h, False, False), h].astype(wide)
+        return mine + first[h, k, 1].astype(wide) + second[h, k].astype(wide)
+
+    def climb(k):
+        for h in range(2):
+            second[h, k] = total(k, h).astype(second.dtype)
+            three[h, k] = send(
+                second.at[h, k], last.at[h, k - 1], target(k, h, False, False),
+                send3.at[h, k - 1], recv3.at[h, k - 1],
+            )
+
+    pass_on(order[0])
+    for before, k in zip(order[:-1], order[1:]):
+        pass_on(k)
+        climb(before)
+    for h in range(2):
+        value = total(0, h)
+        for k in order[:-1]:
+            three[h, k].wait_recv()
+            value = value + last[h, k - 1].astype(wide)
+        out_ref[h] = value.astype(out_ref.dtype)
+    for copy in list(one.values()) + list(two.values()) + list(three.values()):
+        copy.wait_send()
+
+
+def reduce_rows(parts):
+    experts, rows, width = parts.shape
+    half = rows // 2
+    inside = pl.BlockSpec(memory_space=pltpu.VMEM)
+    dma = pltpu.SemaphoreType.DMA
+    mixed = pl.pallas_call(
+        reduce_kernel,
+        out_shape=jax.ShapeDtypeStruct((2, half, width), parts.dtype),
+        in_specs=[inside],
+        out_specs=inside,
+        scratch_shapes=[
+            pltpu.VMEM((2, LAYERS, 2, half, width), parts.dtype),
+            pltpu.VMEM((2, LAYERS, half, width), parts.dtype),
+            pltpu.VMEM((2, LAYERS - 1, half, width), parts.dtype),
+            dma((2, LAYERS, 2)), dma((2, LAYERS, 2)),
+            dma((2, LAYERS)), dma((2, LAYERS)),
+            dma((2, LAYERS - 1)), dma((2, LAYERS - 1)),
+        ],
+        compiler_params=pltpu.CompilerParams(
+            collective_id=1, has_side_effects=True, vmem_limit_bytes=40 * 1024 * 1024
+        ),
+    )(parts.reshape(experts, 2, half, width))
+    return mixed.reshape(rows, width)
+
+
+def tree_body(tokens, expert_ids, combine_weights, w_gate, w_up, w_down):
+    experts = lax.axis_size("expert")
+    tok_rows, model_width = tokens.shape
+    top_count = expert_ids.shape[1]
+    capacity = min(tok_rows, 5 * tok_rows * top_count // (4 * experts))
+    slot_count = experts * capacity
+    out_width = w_down.shape[2]
+    width_share = model_width // SIDE
+    lanes = 128
+    expert_iota = lax.broadcasted_iota(jnp.int32, (1, 1, lanes), 2)
+    chosen = expert_ids[:, :, None] == expert_iota
+    table = jnp.sum(jnp.where(chosen, combine_weights[:, :, None], 0.0), axis=1)
+    place = lax.axis_index("pipe")
+    tok_share = lax.dynamic_slice_in_dim(tokens, place * width_share, width_share, 1)
+    gathered, tables = gather_rows(tok_share, table)
+    mine = lax.broadcasted_iota(jnp.int32, (1, 1, lanes), 2) == lax.axis_index("expert")
+    weights = jnp.sum(jnp.where(mine, tables, 0.0), axis=2)
+    named = weights > 0.0
+    before = lax.broadcasted_iota(jnp.int32, (tok_rows, tok_rows), 0)
+    before = before < lax.broadcasted_iota(jnp.int32, (tok_rows, tok_rows), 1)
+    rank = jnp.dot(named.astype(jnp.bfloat16), before.astype(jnp.bfloat16), preferred_element_type=jnp.float32)
+    slot = jnp.where(named, rank.astype(jnp.int32), -1)
+    marks = slot[:, None, :] == lax.broadcasted_iota(jnp.int32, (1, capacity, 1), 1)
+    row_weight = jnp.sum(jnp.where(marks, weights[:, None, :], 0.0), axis=2)
+    marks = marks.astype(jnp.bfloat16)
+    rows = jnp.einsum("gct,gtd->gcd", marks, gathered, preferred_element_type=jnp.float32)
+    rows = rows.astype(jnp.bfloat16).reshape(slot_count, width_share)
+    gate_acc, up_acc = split_dots(rows, [w_gate[0], w_up[0]])
+    hidden_rows = (jax.nn.silu(gate_acc) * up_acc).astype(jnp.bfloat16)
+    (outputs,) = split_dots(hidden_rows, [w_down[0]])
+    outputs = (outputs * row_weight.reshape(slot_count, 1)).astype(jnp.bfloat16)
+    outputs = outputs.reshape(experts, capacity, out_width)
+    parts = jnp.einsum("gct,gcd->gtd", marks, outputs, preferred_element_type=jnp.float32)
+    return reduce_rows(parts.astype(jnp.bfloat16))
 
 
 def split_dots(mine, weights):
@@ -77,6 +314,7 @@
         P("expert", None, "pipe"),
         P("expert", None, "pipe"),
     )
+    tree = mesh.shape["pipe"] == SIDE and mesh.shape["expert"] == LAYERS * SIDE * SIDE
     return jax.shard_map(
-        body, mesh=mesh, in_specs=placed, out_specs=P("expert", "pipe"), check_vma=False
+        tree_body if tree else body, mesh=mesh, in_specs=placed, out_specs=P("expert", "pipe"), check_vma=False
     )

time: 284 us -> 246 us (0.87)
  Pallas kernels: 0 us -> 174 us
  blocking collectives: 107 us -> 0 us
  waiting for transfers between devices: 103 us -> 0.01 us
  starting transfers between devices: 7.46 us -> 0.57 us
  local copies, waits for them, and re-layouts: 0.4 us -> 3.34 us
    pallas_call x0 -> x2, Pallas kernels: none -> 174 us  [the longest x1 99.2 us: reduce_rows(): pl.pallas_call(reduce_kernel, out_shape=jax.ShapeDtypeStruct((2, half, wi...]
    all_to_all x1 -> x0, blocking collectives: 107 us -> none  [body(): lax.all_to_all(packed, 'expert', split_axis=0, concat_axis=0, tiled=True)]
    all_to_all x1 -> x0, waiting for transfers between devices: 103 us -> none  [body(): lax.all_to_all(outgoing, 'expert', split_axis=0, concat_axis=0, tiled=True)]
    all_to_all x1 -> x0, starting transfers between devices: 6.95 us -> none  [body(): lax.all_to_all(outgoing, 'expert', split_axis=0, concat_axis=0, tiled=True)]
    dot_general x2 -> x3, matrix products: 6.44 us -> 8.84 us  [the longest x1 6.59 us: tree_body(): jnp.einsum('gct,gtd->gcd', marks, gathered, preferred_element_type=jnp.fl...]
  transfers between devices with their start and end apart: 3 -> 2, of which waited for: 1 -> 0; matrix products, arithmetic and copies ran while one was open for 9% -> 11% of each run, Pallas kernels for 0% -> 0%
where the time goes in v2:
time: 246 us; the launch traced here: 243 us
  Pallas kernels  174 us (71%)
  matrix products  61.8 us (25%)
  local copies, waits for them, and re-layouts  3.34 us (1%)
  other arithmetic  2.9 us (1%)
    pallas_call x1, Pallas kernels, reduce_rows(): pl.pallas_call(reduce_kernel, out_shape=jax.ShapeDtypeStruct((2, half, wi...  99.2 us
    pallas_call x1, Pallas kernels, gather_rows(): pl.pallas_call(gather_kernel, out_shape=(jax.ShapeDtypeStruct((experts, 2...  75.1 us
    dot_general x3, matrix products, split_dots(): jnp.dot(other, far, preferred_element_type=jnp.float32)  27.2 us
    dot_general x3, matrix products, split_dots(): total = jnp.dot(mine, own, preferred_element_type=jnp.float32)  25.7 us
    dot_general x1, matrix products, tree_body(): jnp.einsum('gct,gtd->gcd', marks, gathered, preferred_element_type=jnp.fl...  6.59 us
  transfers between devices with their start and end apart: 2, of which 0 were waited for; matrix products, arithmetic and copies ran while one was open for 11% of the time, Pallas kernels for 0%

profile of v2, /device:TPU:14, one launch (start us, length us, event | category | flops | bytes accessed | tf_op | source)
XLA Modules:
  0.0 243.1 jit_solution(8169261033293262692)
XLA Ops:
  0.0 0.0 copy-start
  0.0 0.9 copy.10
  0.9 0.8 copy.9
  1.7 0.0 copy-done
  1.7 0.8 constant_dynamic-slice_fusion
  2.5 1.0 select_reduce_fusion.2.table_ref
  3.5 75.1 %shard_map.64 = (bf16[16,2,64,1792]{3,2,1,0:T(8,128)(2,1)}, f32[16,128,128]{2,1,0:T(8,128)}) custom-call(bf16[2,64,1792]{2,1,0:T(8,128)(2,1)} %bitcast.36, f32[128,128]{1,0:T(8,128)} %select_reduce_fusion.2.table_ref), custom_call_target="tpu_custom_call" | custom-call | tf_op jit(solution)/shard_map/pallas_call | solution.py:99
  78.6 1.6 select_reduce_fusion
  80.1 0.1 fusion.16
  80.3 6.6 %convolution_convert_fusion.1 = bf16[16,80,1792]{2,1,0:T(8,128)(2,1)} fusion(bf16[16,128,1792]{2,1,0:T(8,128)(2,1)} %bitcast.34, s32[16,128]{1,0:T(8,128)S(1)} %fusion.16), kind=kOutput, calls=%fused_computation.3 | convolution fusion | flops 589660160 | bytes 11935744 | tf_op jit(solution)/shard_map/gct,gtd->gcd/dot_general | solution.py:233
  86.9 0.0 collective-permute-start
  86.9 8.0 %fusion.4 = f32[1280,1024]{1,0:T(8,128)S(1)} fusion(bf16[1280,1792]{1,0:T(8,128)(2,1)} %bitcast.2, bf16[1,3584,1024]{2,1,0:T(8,128)(2,1)} %param.10, s32[]{:T(128)S(6)} %select_n.31), kind=kOutput, calls=%fused_computation.8 | convolution fusion | flops 4697620480 | bytes 13500420 | tf_op jit(solution)/shard_map/dot_general | solution.py:252
  94.8 0.0 slice-start.1
  94.9 0.0 slice-start.2
  94.9 10.8 %fusion.8 = f32[1280,1024]{1,0:T(8,128)} fusion(bf16[1280,1792]{1,0:T(8,128)(2,1)} %bitcast.2, bf16[1,3584,1024]{2,1,0:T(8,128)(2,1)} %param.9, s32[]{:T(128)S(6)} %select_n.31), kind=kOutput, calls=%fused_computation.12 | convolution fusion | flops 4697620480 | bytes 13500420 | tf_op jit(solution)/shard_map/dot_general | solution.py:252
  105.7 0.0 collective-permute-done
  105.7 0.0 slice-done
  105.7 0.0 slice-done.1
  105.7 9.2 %fusion.6 = f32[1280,1024]{1,0:T(8,128)} fusion(bf16[1280,1792]{1,0:T(8,128)(2,1)} %collective-permute-done, bf16[1,3584,1024]{2,1,0:T(8,128)(2,1)S(1)} %bitcast.38, s32[]{:T(128)S(6)} %select_n.35), kind=kOutput, calls=%fused_computation.10 | convolution fusion | flops 4697620480 | bytes 13500420 | tf_op jit(solution)/shard_map/dot_general | solution.py:253
  114.8 0.0 slice-done.2
  114.8 0.0 slice-done.3
  114.8 10.3 %multiply_convert_fusion.1 = bf16[1280,1024]{1,0:T(8,128)(2,1)S(1)} fusion(f32[1280,1024]{1,0:T(8,128)S(1)} %fusion.4, f32[1280,1024]{1,0:T(8,128)} %fusion.8, f32[1280,1024]{1,0:T(8,128)} %fusion.6, bf16[1280,1792]{1,0:T(8,128)(2,1)} %collective-permute-done, bf16[1,3584,1024]{2,1,0:T(8,128)(2,1)S(1)} %bitcast.40, s32[]{:T(128)S(6)} %select_n.35), kind=kOutput, calls=%fused_computation.2 | convolution fusion | flops 4708106240 | bytes 26607620 | tf_op jit(solution)/shard_map/dot_general | solution.py:253
  125.2 0.6 collective-permute-start.1
  125.7 0.4 select_reduce_fusion.1
  126.1 0.1 mul.38
  126.2 7.0 %fusion.1 = f32[1280,1792]{1,0:T(8,128)S(1)} fusion(bf16[1280,1024]{1,0:T(8,128)(2,1)S(1)} %multiply_convert_fusion.1, bf16[1,2048,1792]{2,1,0:T(8,128)(2,1)} %param.11, s32[]{:T(128)S(6)} %select_n.36), kind=kOutput, calls=%fused_computation.5 | convolution fusion | flops 4697620480 | bytes 15466500 | tf_op jit(solution)/shard_map/dot_general | solution.py:252
  133.2 0.0 collective-permute-done.1
  133.2 7.8 %multiply_convert_fusion = bf16[1280,1792]{1,0:T(8,128)(2,1)S(1)} fusion(f32[1280,1792]{1,0:T(8,128)S(1)} %fusion.1, bf16[1280,1024]{1,0:T(8,128)(2,1)} %collective-permute-done.1, f32[1280]{0:T(1024)S(1)} %mul.38, bf16[1,2048,1792]{2,1,0:T(8,128)(2,1)} %param.11, s32[]{:T(128)S(6)} %select_n.37), kind=kOutput, calls=%fused_computation | convolution fusion | flops 4704501760 | bytes 20059140 | tf_op jit(solution)/shard_map/dot_general | solution.py:253
  141.0 0.0 copy-start.1
  141.0 2.1 convolution_convert_fusion
  143.1 99.2 %shard_map.65 = bf16[2,64,1792]{2,1,0:T(8,128)(2,1)S(1)} custom-call(bf16[16,2,64,1792]{3,2,1,0:T(8,128)(2,1)S(1)} %bitcast.32), custom_call_target="tpu_custom_call" | custom-call | tf_op jit(solution)/shard_map/pallas_call | solution.py:188
  242.3 0.8 copy.12
  (6 shorter events, 0.0 us)
Async XLA Ops:
  0.0 1.7 copy-start
  86.9 18.8 %collective-permute-start = (bf16[1280,1792]{1,0:T(8,128)(2,1)}, bf16[1280,1792]{1,0:T(8,128)(2,1)}, u32[]{:S(2)}, u32[]{:S(2)}) collective-permute-start(bf16[1280,1792]{1,0:T(8,128)(2,1)} %bitcast.2), channel_id=1, source_target_pairs={{0,16},{16,0},{1,17},{17,1},{2,18},{18,2},{3,19},{19,3},{4,20},{20... | collective-permute-start | bytes 13762568 | tf_op jit(solution)/shard_map/ppermute | solution.py:246
  86.9 18.8 %slice-start = ((s8[7340032]{0:T(1024)(128)(4,1)}), s8[4194304]{0:T(1024)(128)(4,1)S(1)}, s32[]{:S(2)}) async-start(s8[7340032]{0:T(1024)(128)(4,1)} %bitcast.37), calls=%async_computation | async-start | bytes 8388608
  94.8 10.8 %slice-start.1 = ((s8[7340032]{0:T(1024)(128)(4,1)}), s8[3145728]{0:T(1024)(128)(4,1)S(1)}, s32[]{:S(2)}) async-start(s8[7340032]{0:T(1024)(128)(4,1)} %bitcast.37), calls=%async_computation.1 | async-start | bytes 6291456
  94.9 20.0 %slice-start.2 = ((s8[7340032]{0:T(1024)(128)(4,1)}), s8[4194304]{0:T(1024)(128)(4,1)S(1)}, s32[]{:S(2)}) async-start(s8[7340032]{0:T(1024)(128)(4,1)} %bitcast.39), calls=%async_computation.2 | async-start | bytes 8388608
  105.7 9.2 %slice-start.3 = ((s8[7340032]{0:T(1024)(128)(4,1)}), s8[3145728]{0:T(1024)(128)(4,1)S(1)}, s32[]{:S(2)}) async-start(s8[7340032]{0:T(1024)(128)(4,1)} %bitcast.39), calls=%async_computation.3 | async-start | bytes 6291456
  125.2 8.0 %collective-permute-start.1 = (bf16[1280,1024]{1,0:T(8,128)(2,1)S(1)}, bf16[1280,1024]{1,0:T(8,128)(2,1)}, u32[]{:S(2)}, u32[]{:S(2)}) collective-permute-start(bf16[1280,1024]{1,0:T(8,128)(2,1)S(1)} %multiply_convert_fusion.1), channel_id=1, source_target_pairs={{0,16},{16,0},{1,17},{17,1},{2,18},{18,2},{3,19},{19,3},{4,20},{20... | collective-permute-start | bytes 7864328 | tf_op jit(solution)/shard_map/ppermute | solution.py:246
  141.0 102.1 %copy-start.1 = (bf16[128,3584]{1,0:T(8,128)(2,1)S(1)}, bf16[128,3584]{1,0:T(8,128)(2,1)}, u32[]{:S(2)}) copy-start(bf16[128,3584]{1,0:T(8,128)(2,1)} %param.6) | copy-start | bytes 2752516

commit v3 on v2

--- a/solution.py
+++ b/solution.py
@@ -52,17 +52,15 @@
         return copy
 
     order = (2, 0, 1)
-    along = {}
-    for k in range(1, LAYERS):
+    along, near = {}, {}
+
+    def climb(k):
         for j in order:
             along[j, k] = send(own[j], slots[j](me), flat_place(lax.rem(z + k, LAYERS), y, x), j, k, 0)
-    near = {}
 
     def spread(k):
         origin = flat_place(lax.rem(z - k + LAYERS, LAYERS), y, x)
         for j in order:
-            if k:
-                along[j, k].wait_recv()
             source = slots[j](origin) if k else own[j]
             near[j, k] = send(source, slots[j](origin), hops[j][0], j, k, 1)
             send(source, slots[j](origin), hops[j][1], j, k, 2)
@@ -74,13 +72,20 @@
             near[j, k].wait_recv()
             send(slots[j](origin), slots[j](origin), hops[j][1], j, k, 3)
 
+    climb(1)
     spread(0)
     for copy in kept:
         copy.start()
-    for k in range(1, LAYERS):
+    previous = 0
+    for k, later in ((1, 3), (3, 2), (2, None)):
+        for j in order:
+            along[j, k].wait_recv()
+        if later:
+            climb(later)
         spread(k)
-        forward(k - 1)
-    forward(LAYERS - 1)
+        forward(previous)
+        previous = k
+    forward(previous)
     for copy in kept:
         copy.wait()
     for copy in started:
@@ -134,7 +139,8 @@
     wide = jnp.float32
     order = (2, 1, 3, 0)
     one, two, three = {}, {}, {}
-    for k in order:
+
+    def open_layer(k):
         for j in range(2):
             for h in range(2):
                 one[h, k, j] = send(
@@ -166,10 +172,17 @@
                 send3.at[h, k - 1], recv3.at[h, k - 1],
             )
 
+    open_layer(order[0])
+    open_layer(order[1])
     pass_on(order[0])
-    for before, k in zip(order[:-1], order[1:]):
-        pass_on(k)
-        climb(before)
+    open_layer(order[2])
+    pass_on(order[1])
+    climb(order[0])
+    open_layer(order[3])
+    pass_on(order[2])
+    climb(order[1])
+    pass_on(order[3])
+    climb(order[2])
     for h in range(2):
         value = total(0, h)
         for k in order[:-1]:

time: 246 us -> 218 us (0.89)
  Pallas kernels: 174 us -> 147 us
    pallas_call x1, Pallas kernels: 99.2 us -> 70 us  [reduce_rows(): pl.pallas_call(reduce_kernel, out_shape=jax.ShapeDtypeStruct((2, half, wi...]
  transfers between devices with their start and end apart: 2 -> 2, of which waited for: 0 -> 0; matrix products, arithmetic and copies ran while one was open for 11% -> 12% of each run, Pallas kernels for 0% -> 0%
where the time goes in v3:
time: 218 us; the launch traced here: 215 us
  Pallas kernels  147 us (67%)
  matrix products  61.8 us (28%)
  local copies, waits for them, and re-layouts  3.34 us (2%)
  other arithmetic  2.9 us (1%)
    pallas_call x1, Pallas kernels, gather_rows(): pl.pallas_call(gather_kernel, out_shape=(jax.ShapeDtypeStruct((experts, 2...  76.6 us
    pallas_call x1, Pallas kernels, reduce_rows(): pl.pallas_call(reduce_kernel, out_shape=jax.ShapeDtypeStruct((2, half, wi...  70 us
    dot_general x3, matrix products, split_dots(): jnp.dot(other, far, preferred_element_type=jnp.float32)  27.2 us
    dot_general x3, matrix products, split_dots(): total = jnp.dot(mine, own, preferred_element_type=jnp.float32)  25.7 us
    dot_general x1, matrix products, tree_body(): jnp.einsum('gct,gtd->gcd', marks, gathered, preferred_element_type=jnp.fl...  6.59 us
  transfers between devices with their start and end apart: 2, of which 0 were waited for; matrix products, arithmetic and copies ran while one was open for 12% of the time, Pallas kernels for 0%

profile of v3, /device:TPU:14, one launch (start us, length us, event | category | flops | bytes accessed | tf_op | source)
XLA Modules:
  0.0 215.3 jit_solution(11703961403711104981)
XLA Ops:
  0.0 0.0 copy-start
  0.0 0.9 copy.10
  0.9 0.8 copy.9
  1.7 0.0 copy-done
  1.7 0.8 constant_dynamic-slice_fusion
  2.5 1.0 select_reduce_fusion.2.table_ref
  3.5 76.6 %shard_map.64 = (bf16[16,2,64,1792]{3,2,1,0:T(8,128)(2,1)}, f32[16,128,128]{2,1,0:T(8,128)}) custom-call(bf16[2,64,1792]{2,1,0:T(8,128)(2,1)} %bitcast.36, f32[128,128]{1,0:T(8,128)} %select_reduce_fusion.2.table_ref), custom_call_target="tpu_custom_call" | custom-call | tf_op jit(solution)/shard_map/pallas_call | solution.py:104
  80.0 1.6 select_reduce_fusion
  81.6 0.1 fusion.16
  81.7 6.6 %convolution_convert_fusion.1 = bf16[16,80,1792]{2,1,0:T(8,128)(2,1)} fusion(bf16[16,128,1792]{2,1,0:T(8,128)(2,1)} %bitcast.34, s32[16,128]{1,0:T(8,128)S(1)} %fusion.16), kind=kOutput, calls=%fused_computation.3 | convolution fusion | flops 589660160 | bytes 11935744 | tf_op jit(solution)/shard_map/gct,gtd->gcd/dot_general | solution.py:246
  88.3 0.0 collective-permute-start
  88.3 8.0 %fusion.4 = f32[1280,1024]{1,0:T(8,128)S(1)} fusion(bf16[1280,1792]{1,0:T(8,128)(2,1)} %bitcast.2, bf16[1,3584,1024]{2,1,0:T(8,128)(2,1)} %param.10, s32[]{:T(128)S(6)} %select_n.31), kind=kOutput, calls=%fused_computation.8 | convolution fusion | flops 4697620480 | bytes 13500420 | tf_op jit(solution)/shard_map/dot_general | solution.py:265
  96.3 0.0 slice-start.1
  96.3 0.0 slice-start.2
  96.3 10.8 %fusion.8 = f32[1280,1024]{1,0:T(8,128)} fusion(bf16[1280,1792]{1,0:T(8,128)(2,1)} %bitcast.2, bf16[1,3584,1024]{2,1,0:T(8,128)(2,1)} %param.9, s32[]{:T(128)S(6)} %select_n.31), kind=kOutput, calls=%fused_computation.12 | convolution fusion | flops 4697620480 | bytes 13500420 | tf_op jit(solution)/shard_map/dot_general | solution.py:265
  107.1 0.0 collective-permute-done
  107.1 0.0 slice-done
  107.2 0.0 slice-done.1
  107.2 9.2 %fusion.6 = f32[1280,1024]{1,0:T(8,128)} fusion(bf16[1280,1792]{1,0:T(8,128)(2,1)} %collective-permute-done, bf16[1,3584,1024]{2,1,0:T(8,128)(2,1)S(1)} %bitcast.38, s32[]{:T(128)S(6)} %select_n.35), kind=kOutput, calls=%fused_computation.10 | convolution fusion | flops 4697620480 | bytes 13500420 | tf_op jit(solution)/shard_map/dot_general | solution.py:266
  116.3 0.0 slice-done.2
  116.3 10.3 %multiply_convert_fusion.1 = bf16[1280,1024]{1,0:T(8,128)(2,1)S(1)} fusion(f32[1280,1024]{1,0:T(8,128)S(1)} %fusion.4, f32[1280,1024]{1,0:T(8,128)} %fusion.8, f32[1280,1024]{1,0:T(8,128)} %fusion.6, bf16[1280,1792]{1,0:T(8,128)(2,1)} %collective-permute-done, bf16[1,3584,1024]{2,1,0:T(8,128)(2,1)S(1)} %bitcast.40, s32[]{:T(128)S(6)} %select_n.35), kind=kOutput, calls=%fused_computation.2 | convolution fusion | flops 4708106240 | bytes 26607620 | tf_op jit(solution)/shard_map/dot_general | solution.py:266
  126.7 0.6 collective-permute-start.1
  127.2 0.4 select_reduce_fusion.1
  127.6 0.1 mul.38
  127.7 7.0 %fusion.1 = f32[1280,1792]{1,0:T(8,128)S(1)} fusion(bf16[1280,1024]{1,0:T(8,128)(2,1)S(1)} %multiply_convert_fusion.1, bf16[1,2048,1792]{2,1,0:T(8,128)(2,1)} %param.11, s32[]{:T(128)S(6)} %select_n.36), kind=kOutput, calls=%fused_computation.5 | convolution fusion | flops 4697620480 | bytes 15466500 | tf_op jit(solution)/shard_map/dot_general | solution.py:265
  134.6 0.0 collective-permute-done.1
  134.7 7.8 %multiply_convert_fusion = bf16[1280,1792]{1,0:T(8,128)(2,1)S(1)} fusion(f32[1280,1792]{1,0:T(8,128)S(1)} %fusion.1, bf16[1280,1024]{1,0:T(8,128)(2,1)} %collective-permute-done.1, f32[1280]{0:T(1024)S(1)} %mul.38, bf16[1,2048,1792]{2,1,0:T(8,128)(2,1)} %param.11, s32[]{:T(128)S(6)} %select_n.37), kind=kOutput, calls=%fused_computation | convolution fusion | flops 4704501760 | bytes 20059140 | tf_op jit(solution)/shard_map/dot_general | solution.py:266
  142.4 0.0 copy-start.1
  142.4 2.1 convolution_convert_fusion
  144.6 70.0 %shard_map.65 = bf16[2,64,1792]{2,1,0:T(8,128)(2,1)S(1)} custom-call(bf16[16,2,64,1792]{3,2,1,0:T(8,128)(2,1)S(1)} %bitcast.32), custom_call_target="tpu_custom_call" | custom-call | tf_op jit(solution)/shard_map/pallas_call | solution.py:201
  214.6 0.8 copy.12
  215.3 0.0 copy-done.1
  (6 shorter events, 0.0 us)
Async XLA Ops:
  0.0 1.7 copy-start
  88.3 18.8 %collective-permute-start = (bf16[1280,1792]{1,0:T(8,128)(2,1)}, bf16[1280,1792]{1,0:T(8,128)(2,1)}, u32[]{:S(2)}, u32[]{:S(2)}) collective-permute-start(bf16[1280,1792]{1,0:T(8,128)(2,1)} %bitcast.2), channel_id=1, source_target_pairs={{0,16},{16,0},{1,17},{17,1},{2,18},{18,2},{3,19},{19,3},{4,20},{20... | collective-permute-start | bytes 13762568 | tf_op jit(solution)/shard_map/ppermute | solution.py:259
  88.3 18.8 %slice-start = ((s8[7340032]{0:T(1024)(128)(4,1)}), s8[4194304]{0:T(1024)(128)(4,1)S(1)}, s32[]{:S(2)}) async-start(s8[7340032]{0:T(1024)(128)(4,1)} %bitcast.37), calls=%async_computation | async-start | bytes 8388608
  96.3 10.8 %slice-start.1 = ((s8[7340032]{0:T(1024)(128)(4,1)}), s8[3145728]{0:T(1024)(128)(4,1)S(1)}, s32[]{:S(2)}) async-start(s8[7340032]{0:T(1024)(128)(4,1)} %bitcast.37), calls=%async_computation.1 | async-start | bytes 6291456
  96.3 20.0 %slice-start.2 = ((s8[7340032]{0:T(1024)(128)(4,1)}), s8[4194304]{0:T(1024)(128)(4,1)S(1)}, s32[]{:S(2)}) async-start(s8[7340032]{0:T(1024)(128)(4,1)} %bitcast.39), calls=%async_computation.2 | async-start | bytes 8388608
  107.1 9.2 %slice-start.3 = ((s8[7340032]{0:T(1024)(128)(4,1)}), s8[3145728]{0:T(1024)(128)(4,1)S(1)}, s32[]{:S(2)}) async-start(s8[7340032]{0:T(1024)(128)(4,1)} %bitcast.39), calls=%async_computation.3 | async-start | bytes 6291456
  126.7 8.0 %collective-permute-start.1 = (bf16[1280,1024]{1,0:T(8,128)(2,1)S(1)}, bf16[1280,1024]{1,0:T(8,128)(2,1)}, u32[]{:S(2)}, u32[]{:S(2)}) collective-permute-start(bf16[1280,1024]{1,0:T(8,128)(2,1)S(1)} %multiply_convert_fusion.1), channel_id=1, source_target_pairs={{0,16},{16,0},{1,17},{17,1},{2,18},{18,2},{3,19},{19,3},{4,20},{20... | collective-permute-start | bytes 7864328 | tf_op jit(solution)/shard_map/ppermute | solution.py:259
  142.4 72.9 %copy-start.1 = (bf16[128,3584]{1,0:T(8,128)(2,1)S(1)}, bf16[128,3584]{1,0:T(8,128)(2,1)}, u32[]{:S(2)}) copy-start(bf16[128,3584]{1,0:T(8,128)(2,1)} %param.6) | copy-start | bytes 2752516

commit v4 on v3

--- a/solution.py
+++ b/solution.py
@@ -105,7 +105,7 @@
         gather_kernel,
         out_shape=(
             jax.ShapeDtypeStruct((experts, 2, half, width), tokens.dtype),
-            jax.ShapeDtypeStruct((experts, rows, table.shape[1]), table.dtype),
+            jax.ShapeDtypeStruct((experts,) + table.shape, table.dtype),
         ),
         in_specs=[anywhere, anywhere],
         out_specs=(anywhere, anywhere),
@@ -226,15 +226,13 @@
     slot_count = experts * capacity
     out_width = w_down.shape[2]
     width_share = model_width // SIDE
-    lanes = 128
-    expert_iota = lax.broadcasted_iota(jnp.int32, (1, 1, lanes), 2)
-    chosen = expert_ids[:, :, None] == expert_iota
-    table = jnp.sum(jnp.where(chosen, combine_weights[:, :, None], 0.0), axis=1)
+    expert_iota = lax.broadcasted_iota(jnp.int32, (1, experts, 1), 1)
+    chosen = expert_ids.T[:, None, :] == expert_iota
+    table = jnp.sum(jnp.where(chosen, combine_weights.T[:, None, :], 0.0), axis=0)
     place = lax.axis_index("pipe")
     tok_share = lax.dynamic_slice_in_dim(tokens, place * width_share, width_share, 1)
     gathered, tables = gather_rows(tok_share, table)
-    mine = lax.broadcasted_iota(jnp.int32, (1, 1, lanes), 2) == lax.axis_index("expert")
-    weights = jnp.sum(jnp.where(mine, tables, 0.0), axis=2)
+    weights = lax.dynamic_index_in_dim(tables, lax.axis_index("expert"), 1, keepdims=False)
     named = weights > 0.0
     before = lax.broadcasted_iota(jnp.int32, (tok_rows, tok_rows), 0)
     before = before < lax.broadcasted_iota(jnp.int32, (tok_rows, tok_rows), 1)

time: 218 us -> 209 us (0.959)
  Pallas kernels: 147 us -> 138 us
    pallas_call x1, Pallas kernels: 76.6 us -> 66.7 us  [gather_rows(): pl.pallas_call(gather_kernel, out_shape=(jax.ShapeDtypeStruct((experts, 2...]
  transfers between devices with their start and end apart: 2 -> 2, of which waited for: 0 -> 0; matrix products, arithmetic and copies ran while one was open for 12% -> 13% of each run, Pallas kernels for 0% -> 0%
where the time goes in v4:
time: 209 us; the launch traced here: 206 us
  Pallas kernels  138 us (66%)
  matrix products  61.8 us (30%)
  local copies, waits for them, and re-layouts  3.7 us (2%)
    pallas_call x1, Pallas kernels, reduce_rows(): pl.pallas_call(reduce_kernel, out_shape=jax.ShapeDtypeStruct((2, half, wi...  71.2 us
    pallas_call x1, Pallas kernels, gather_rows(): pl.pallas_call(gather_kernel, out_shape=(jax.ShapeDtypeStruct((experts, 2...  66.7 us
    dot_general x3, matrix products, split_dots(): jnp.dot(other, far, preferred_element_type=jnp.float32)  27.2 us
    dot_general x3, matrix products, split_dots(): total = jnp.dot(mine, own, preferred_element_type=jnp.float32)  25.7 us
    dot_general x1, matrix products, tree_body(): jnp.einsum('gct,gtd->gcd', marks, gathered, preferred_element_type=jnp.fl...  6.59 us
  transfers between devices with their start and end apart: 2, of which 0 were waited for; matrix products, arithmetic and copies ran while one was open for 13% of the time, Pallas kernels for 0%

profile of v4, /device:TPU:14, one launch (start us, length us, event | category | flops | bytes accessed | tf_op | source)
XLA Modules:
  0.0 205.9 jit_solution(13778289238859533545)
XLA Ops:
  0.0 0.0 copy-start
  0.0 1.2 copy-done
  1.2 0.8 constant_dynamic-slice_fusion.1
  2.0 1.3 select_reduce_fusion.1.table_ref
  3.3 66.7 %shard_map.64 = (bf16[16,2,64,1792]{3,2,1,0:T(8,128)(2,1)}, f32[16,16,128]{2,1,0:T(8,128)}) custom-call(bf16[2,64,1792]{2,1,0:T(8,128)(2,1)} %bitcast.39, f32[16,128]{1,0:T(8,128)} %select_reduce_fusion.1.table_ref), custom_call_target="tpu_custom_call" | custom-call | tf_op jit(solution)/shard_map/pallas_call | solution.py:104
  70.0 0.9 constant_dynamic-slice_fusion
  70.9 0.1 fusion.16
  71.0 6.6 %convolution_convert_fusion.1 = bf16[16,80,1792]{2,1,0:T(8,128)(2,1)} fusion(bf16[16,128,1792]{2,1,0:T(8,128)(2,1)} %bitcast.37, s32[16,128]{1,0:T(8,128)S(1)} %fusion.16), kind=kOutput, calls=%fused_computation.3 | convolution fusion | flops 589660160 | bytes 11935744 | tf_op jit(solution)/shard_map/gct,gtd->gcd/dot_general | solution.py:244
  77.6 0.0 collective-permute-start
  77.6 0.0 slice-start
  77.6 8.0 %fusion.4 = f32[1280,1024]{1,0:T(8,128)S(1)} fusion(bf16[1280,1792]{1,0:T(8,128)(2,1)} %bitcast.5, bf16[1,3584,1024]{2,1,0:T(8,128)(2,1)} %param.10, s32[]{:T(128)S(6)} %select_n.31), kind=kOutput, calls=%fused_computation.8 | convolution fusion | flops 4697620480 | bytes 13500420 | tf_op jit(solution)/shard_map/dot_general | solution.py:263
  85.6 0.0 slice-start.1
  85.6 0.0 slice-start.2
  85.6 10.8 %fusion.8 = f32[1280,1024]{1,0:T(8,128)} fusion(bf16[1280,1792]{1,0:T(8,128)(2,1)} %bitcast.5, bf16[1,3584,1024]{2,1,0:T(8,128)(2,1)} %param.9, s32[]{:T(128)S(6)} %select_n.31), kind=kOutput, calls=%fused_computation.12 | convolution fusion | flops 4697620480 | bytes 13500420 | tf_op jit(solution)/shard_map/dot_general | solution.py:263
  96.4 0.0 collective-permute-done
  96.4 0.0 slice-done
  96.4 0.0 slice-done.1
  96.5 9.2 %fusion.6 = f32[1280,1024]{1,0:T(8,128)} fusion(bf16[1280,1792]{1,0:T(8,128)(2,1)} %collective-permute-done, bf16[1,3584,1024]{2,1,0:T(8,128)(2,1)S(1)} %bitcast.45, s32[]{:T(128)S(6)} %select_n.35), kind=kOutput, calls=%fused_computation.10 | convolution fusion | flops 4697620480 | bytes 13500420 | tf_op jit(solution)/shard_map/dot_general | solution.py:264
  105.6 0.0 slice-done.2
  105.6 0.0 slice-done.3
  105.6 10.3 %multiply_convert_fusion.1 = bf16[1280,1024]{1,0:T(8,128)(2,1)S(1)} fusion(f32[1280,1024]{1,0:T(8,128)S(1)} %fusion.4, f32[1280,1024]{1,0:T(8,128)} %fusion.8, f32[1280,1024]{1,0:T(8,128)} %fusion.6, bf16[1280,1792]{1,0:T(8,128)(2,1)} %collective-permute-done, bf16[1,3584,1024]{2,1,0:T(8,128)(2,1)S(1)} %bitcast.47, s32[]{:T(128)S(6)} %select_n.35), kind=kOutput, calls=%fused_computation.2 | convolution fusion | flops 4708106240 | bytes 26607620 | tf_op jit(solution)/shard_map/dot_general | solution.py:264
  115.9 0.6 collective-permute-start.1
  116.5 0.4 select_reduce_fusion
  116.9 0.1 mul.38
  116.9 7.0 %fusion.1 = f32[1280,1792]{1,0:T(8,128)S(1)} fusion(bf16[1280,1024]{1,0:T(8,128)(2,1)S(1)} %multiply_convert_fusion.1, bf16[1,2048,1792]{2,1,0:T(8,128)(2,1)} %param.11, s32[]{:T(128)S(6)} %select_n.36), kind=kOutput, calls=%fused_computation.5 | convolution fusion | flops 4697620480 | bytes 15466500 | tf_op jit(solution)/shard_map/dot_general | solution.py:263
  123.9 0.0 collective-permute-done.1
  123.9 7.8 %multiply_convert_fusion = bf16[1280,1792]{1,0:T(8,128)(2,1)S(1)} fusion(f32[1280,1792]{1,0:T(8,128)S(1)} %fusion.1, bf16[1280,1024]{1,0:T(8,128)(2,1)} %collective-permute-done.1, f32[1280]{0:T(1024)S(1)} %mul.38, bf16[1,2048,1792]{2,1,0:T(8,128)(2,1)} %param.11, s32[]{:T(128)S(6)} %select_n.37), kind=kOutput, calls=%fused_computation | convolution fusion | flops 4704501760 | bytes 20059140 | tf_op jit(solution)/shard_map/dot_general | solution.py:264
  131.7 0.0 copy-start.1
  131.7 2.1 %convolution_convert_fusion = bf16[16,128,1792]{2,1,0:T(8,128)(2,1)S(1)} fusion(bf16[16,80,1792]{2,1,0:T(8,128)(2,1)S(1)} %bitcast.38, s32[16,128]{1,0:T(8,128)S(1)} %fusion.16), kind=kOutput, calls=%fused_computation.1 | convolution fusion | flops 591036416 | bytes 11935744 | tf_op jit(solution)/shard_map/gct,gcd->gtd/dot_general | solution.py:251
  133.8 71.2 %shard_map.65 = bf16[2,64,1792]{2,1,0:T(8,128)(2,1)S(1)} custom-call(bf16[16,2,64,1792]{3,2,1,0:T(8,128)(2,1)S(1)} %bitcast.35), custom_call_target="tpu_custom_call" | custom-call | tf_op jit(solution)/shard_map/pallas_call | solution.py:201
  205.1 0.8 copy.8
  205.8 0.0 copy-done.1
  (3 shorter events, 0.0 us)
Async XLA Ops:
  0.0 1.2 copy-start
  77.6 18.8 %collective-permute-start = (bf16[1280,1792]{1,0:T(8,128)(2,1)}, bf16[1280,1792]{1,0:T(8,128)(2,1)}, u32[]{:S(2)}, u32[]{:S(2)}) collective-permute-start(bf16[1280,1792]{1,0:T(8,128)(2,1)} %bitcast.5), channel_id=1, source_target_pairs={{0,16},{16,0},{1,17},{17,1},{2,18},{18,2},{3,19},{19,3},{4,20},{20... | collective-permute-start | bytes 13762568 | tf_op jit(solution)/shard_map/ppermute | solution.py:257
  77.6 18.8 %slice-start = ((s8[7340032]{0:T(1024)(128)(4,1)}), s8[4194304]{0:T(1024)(128)(4,1)S(1)}, s32[]{:S(2)}) async-start(s8[7340032]{0:T(1024)(128)(4,1)} %bitcast.44), calls=%async_computation | async-start | bytes 8388608
  85.6 10.8 %slice-start.1 = ((s8[7340032]{0:T(1024)(128)(4,1)}), s8[3145728]{0:T(1024)(128)(4,1)S(1)}, s32[]{:S(2)}) async-start(s8[7340032]{0:T(1024)(128)(4,1)} %bitcast.44), calls=%async_computation.1 | async-start | bytes 6291456
  85.6 20.0 %slice-start.2 = ((s8[7340032]{0:T(1024)(128)(4,1)}), s8[4194304]{0:T(1024)(128)(4,1)S(1)}, s32[]{:S(2)}) async-start(s8[7340032]{0:T(1024)(128)(4,1)} %bitcast.46), calls=%async_computation.2 | async-start | bytes 8388608
  96.4 9.2 %slice-start.3 = ((s8[7340032]{0:T(1024)(128)(4,1)}), s8[3145728]{0:T(1024)(128)(4,1)S(1)}, s32[]{:S(2)}) async-start(s8[7340032]{0:T(1024)(128)(4,1)} %bitcast.46), calls=%async_computation.3 | async-start | bytes 6291456
  115.9 8.0 %collective-permute-start.1 = (bf16[1280,1024]{1,0:T(8,128)(2,1)S(1)}, bf16[1280,1024]{1,0:T(8,128)(2,1)}, u32[]{:S(2)}, u32[]{:S(2)}) collective-permute-start(bf16[1280,1024]{1,0:T(8,128)(2,1)S(1)} %multiply_convert_fusion.1), channel_id=1, source_target_pairs={{0,16},{16,0},{1,17},{17,1},{2,18},{18,2},{3,19},{19,3},{4,20},{20... | collective-permute-start | bytes 7864328 | tf_op jit(solution)/shard_map/ppermute | solution.py:257
  131.7 74.1 %copy-start.1 = (bf16[128,3584]{1,0:T(8,128)(2,1)S(1)}, bf16[128,3584]{1,0:T(8,128)(2,1)}, u32[]{:S(2)}) copy-start(bf16[128,3584]{1,0:T(8,128)(2,1)} %param.6) | copy-start | bytes 2752516

commit v5 on v4

--- a/solution.py
+++ b/solution.py
@@ -73,11 +73,12 @@
             send(slots[j](origin), slots[j](origin), hops[j][1], j, k, 3)
 
     climb(1)
+    climb(3)
     spread(0)
     for copy in kept:
         copy.start()
     previous = 0
-    for k, later in ((1, 3), (3, 2), (2, None)):
+    for k, later in ((1, None), (3, 2), (2, None)):
         for j in order:
             along[j, k].wait_recv()
         if later:

time: 209 us -> 209 us (level)
  no operation moved by 1% of the time
where the time goes in v5:
time: 209 us; the launch traced here: 205 us
  Pallas kernels  137 us (66%)
  matrix products  61.8 us (30%)
  local copies, waits for them, and re-layouts  3.7 us (2%)
    pallas_call x1, Pallas kernels, reduce_rows(): pl.pallas_call(reduce_kernel, out_shape=jax.ShapeDtypeStruct((2, half, wi...  70.5 us
    pallas_call x1, Pallas kernels, gather_rows(): pl.pallas_call(gather_kernel, out_shape=(jax.ShapeDtypeStruct((experts, 2...  66.7 us
    dot_general x3, matrix products, split_dots(): jnp.dot(other, far, preferred_element_type=jnp.float32)  27.2 us
    dot_general x3, matrix products, split_dots(): total = jnp.dot(mine, own, preferred_element_type=jnp.float32)  25.7 us
    dot_general x1, matrix products, tree_body(): jnp.einsum('gct,gtd->gcd', marks, gathered, preferred_element_type=jnp.fl...  6.59 us
  transfers between devices with their start and end apart: 2, of which 0 were waited for; matrix products, arithmetic and copies ran while one was open for 13% of the time, Pallas kernels for 0%

profile of v5, /device:TPU:14, one launch (start us, length us, event | category | flops | bytes accessed | tf_op | source)
XLA Modules:
  0.0 205.1 jit_solution(16642171576988580632)
XLA Ops:
  0.0 0.0 copy-start
  0.0 1.2 copy-done
  1.2 0.8 constant_dynamic-slice_fusion.1
  2.0 1.3 select_reduce_fusion.1.table_ref
  3.3 66.7 %shard_map.64 = (bf16[16,2,64,1792]{3,2,1,0:T(8,128)(2,1)}, f32[16,16,128]{2,1,0:T(8,128)}) custom-call(bf16[2,64,1792]{2,1,0:T(8,128)(2,1)} %bitcast.39, f32[16,128]{1,0:T(8,128)} %select_reduce_fusion.1.table_ref), custom_call_target="tpu_custom_call" | custom-call | tf_op jit(solution)/shard_map/pallas_call | solution.py:105
  70.0 0.9 constant_dynamic-slice_fusion
  70.9 0.1 fusion.16
  71.0 6.6 %convolution_convert_fusion.1 = bf16[16,80,1792]{2,1,0:T(8,128)(2,1)} fusion(bf16[16,128,1792]{2,1,0:T(8,128)(2,1)} %bitcast.37, s32[16,128]{1,0:T(8,128)S(1)} %fusion.16), kind=kOutput, calls=%fused_computation.3 | convolution fusion | flops 589660160 | bytes 11935744 | tf_op jit(solution)/shard_map/gct,gtd->gcd/dot_general | solution.py:245
  77.6 0.0 collective-permute-start
  77.6 0.0 slice-start
  77.6 8.0 %fusion.4 = f32[1280,1024]{1,0:T(8,128)S(1)} fusion(bf16[1280,1792]{1,0:T(8,128)(2,1)} %bitcast.5, bf16[1,3584,1024]{2,1,0:T(8,128)(2,1)} %param.10, s32[]{:T(128)S(6)} %select_n.31), kind=kOutput, calls=%fused_computation.8 | convolution fusion | flops 4697620480 | bytes 13500420 | tf_op jit(solution)/shard_map/dot_general | solution.py:264
  85.6 0.0 slice-start.1
  85.6 0.0 slice-start.2
  85.6 10.8 %fusion.8 = f32[1280,1024]{1,0:T(8,128)} fusion(bf16[1280,1792]{1,0:T(8,128)(2,1)} %bitcast.5, bf16[1,3584,1024]{2,1,0:T(8,128)(2,1)} %param.9, s32[]{:T(128)S(6)} %select_n.31), kind=kOutput, calls=%fused_computation.12 | convolution fusion | flops 4697620480 | bytes 13500420 | tf_op jit(solution)/shard_map/dot_general | solution.py:264
  96.4 0.0 collective-permute-done
  96.4 0.0 slice-done
  96.4 0.0 slice-done.1
  96.5 9.2 %fusion.6 = f32[1280,1024]{1,0:T(8,128)} fusion(bf16[1280,1792]{1,0:T(8,128)(2,1)} %collective-permute-done, bf16[1,3584,1024]{2,1,0:T(8,128)(2,1)S(1)} %bitcast.45, s32[]{:T(128)S(6)} %select_n.35), kind=kOutput, calls=%fused_computation.10 | convolution fusion | flops 4697620480 | bytes 13500420 | tf_op jit(solution)/shard_map/dot_general | solution.py:265
  105.6 0.0 slice-done.2
  105.6 0.0 slice-done.3
  105.6 10.3 %multiply_convert_fusion.1 = bf16[1280,1024]{1,0:T(8,128)(2,1)S(1)} fusion(f32[1280,1024]{1,0:T(8,128)S(1)} %fusion.4, f32[1280,1024]{1,0:T(8,128)} %fusion.8, f32[1280,1024]{1,0:T(8,128)} %fusion.6, bf16[1280,1792]{1,0:T(8,128)(2,1)} %collective-permute-done, bf16[1,3584,1024]{2,1,0:T(8,128)(2,1)S(1)} %bitcast.47, s32[]{:T(128)S(6)} %select_n.35), kind=kOutput, calls=%fused_computation.2 | convolution fusion | flops 4708106240 | bytes 26607620 | tf_op jit(solution)/shard_map/dot_general | solution.py:265
  115.9 0.6 collective-permute-start.1
  116.5 0.4 select_reduce_fusion
  116.9 0.1 mul.38
  116.9 7.0 %fusion.1 = f32[1280,1792]{1,0:T(8,128)S(1)} fusion(bf16[1280,1024]{1,0:T(8,128)(2,1)S(1)} %multiply_convert_fusion.1, bf16[1,2048,1792]{2,1,0:T(8,128)(2,1)} %param.11, s32[]{:T(128)S(6)} %select_n.36), kind=kOutput, calls=%fused_computation.5 | convolution fusion | flops 4697620480 | bytes 15466500 | tf_op jit(solution)/shard_map/dot_general | solution.py:264
  123.9 0.0 collective-permute-done.1
  123.9 7.8 %multiply_convert_fusion = bf16[1280,1792]{1,0:T(8,128)(2,1)S(1)} fusion(f32[1280,1792]{1,0:T(8,128)S(1)} %fusion.1, bf16[1280,1024]{1,0:T(8,128)(2,1)} %collective-permute-done.1, f32[1280]{0:T(1024)S(1)} %mul.38, bf16[1,2048,1792]{2,1,0:T(8,128)(2,1)} %param.11, s32[]{:T(128)S(6)} %select_n.37), kind=kOutput, calls=%fused_computation | convolution fusion | flops 4704501760 | bytes 20059140 | tf_op jit(solution)/shard_map/dot_general | solution.py:265
  131.7 0.0 copy-start.1
  131.7 2.1 %convolution_convert_fusion = bf16[16,128,1792]{2,1,0:T(8,128)(2,1)S(1)} fusion(bf16[16,80,1792]{2,1,0:T(8,128)(2,1)S(1)} %bitcast.38, s32[16,128]{1,0:T(8,128)S(1)} %fusion.16), kind=kOutput, calls=%fused_computation.1 | convolution fusion | flops 591036416 | bytes 11935744 | tf_op jit(solution)/shard_map/gct,gcd->gtd/dot_general | solution.py:252
  133.8 70.5 %shard_map.65 = bf16[2,64,1792]{2,1,0:T(8,128)(2,1)S(1)} custom-call(bf16[16,2,64,1792]{3,2,1,0:T(8,128)(2,1)S(1)} %bitcast.35), custom_call_target="tpu_custom_call" | custom-call | tf_op jit(solution)/shard_map/pallas_call | solution.py:202
  204.3 0.8 copy.8
  205.1 0.0 copy-done.1
  (3 shorter events, 0.0 us)
Async XLA Ops:
  0.0 1.2 copy-start
  77.6 18.8 %collective-permute-start = (bf16[1280,1792]{1,0:T(8,128)(2,1)}, bf16[1280,1792]{1,0:T(8,128)(2,1)}, u32[]{:S(2)}, u32[]{:S(2)}) collective-permute-start(bf16[1280,1792]{1,0:T(8,128)(2,1)} %bitcast.5), channel_id=1, source_target_pairs={{0,16},{16,0},{1,17},{17,1},{2,18},{18,2},{3,19},{19,3},{4,20},{20... | collective-permute-start | bytes 13762568 | tf_op jit(solution)/shard_map/ppermute | solution.py:258
  77.6 18.8 %slice-start = ((s8[7340032]{0:T(1024)(128)(4,1)}), s8[4194304]{0:T(1024)(128)(4,1)S(1)}, s32[]{:S(2)}) async-start(s8[7340032]{0:T(1024)(128)(4,1)} %bitcast.44), calls=%async_computation | async-start | bytes 8388608
  85.6 10.8 %slice-start.1 = ((s8[7340032]{0:T(1024)(128)(4,1)}), s8[3145728]{0:T(1024)(128)(4,1)S(1)}, s32[]{:S(2)}) async-start(s8[7340032]{0:T(1024)(128)(4,1)} %bitcast.44), calls=%async_computation.1 | async-start | bytes 6291456
  85.6 20.0 %slice-start.2 = ((s8[7340032]{0:T(1024)(128)(4,1)}), s8[4194304]{0:T(1024)(128)(4,1)S(1)}, s32[]{:S(2)}) async-start(s8[7340032]{0:T(1024)(128)(4,1)} %bitcast.46), calls=%async_computation.2 | async-start | bytes 8388608
  96.4 9.2 %slice-start.3 = ((s8[7340032]{0:T(1024)(128)(4,1)}), s8[3145728]{0:T(1024)(128)(4,1)S(1)}, s32[]{:S(2)}) async-start(s8[7340032]{0:T(1024)(128)(4,1)} %bitcast.46), calls=%async_computation.3 | async-start | bytes 6291456
  115.9 8.0 %collective-permute-start.1 = (bf16[1280,1024]{1,0:T(8,128)(2,1)S(1)}, bf16[1280,1024]{1,0:T(8,128)(2,1)}, u32[]{:S(2)}, u32[]{:S(2)}) collective-permute-start(bf16[1280,1024]{1,0:T(8,128)(2,1)S(1)} %multiply_convert_fusion.1), channel_id=1, source_target_pairs={{0,16},{16,0},{1,17},{17,1},{2,18},{18,2},{3,19},{19,3},{4,20},{20... | collective-permute-start | bytes 7864328 | tf_op jit(solution)/shard_map/ppermute | solution.py:258
  131.7 73.4 %copy-start.1 = (bf16[128,3584]{1,0:T(8,128)(2,1)S(1)}, bf16[128,3584]{1,0:T(8,128)(2,1)}, u32[]{:S(2)}) copy-start(bf16[128,3584]{1,0:T(8,128)(2,1)} %param.6) | copy-start | bytes 2752516
